TPU v7x, 512 devices: a whole 4x4x16 slice. The times are simulated.
512 devices in a mesh: out: 16 (over x, y_hi, core), in: 32 (over z, y_lo).
Axes of the slice: x: 4, y: 4 (y_hi: 2, y_lo: 2; y = y_hi * 2 + y_lo), z: 16, core: 2. Of those that a mesh axis runs over, the one named last changes fastest.
Arguments:
- kernel_weights: bfloat16 [2, 16384, 32768], P(None, 'out', 'in'), may hold values from -0.03125 to 0.03125
- mode_field: bfloat16 [32768, 1024], P('in', 'out'), may hold values from -6 to 6
- diff_blocks: bfloat16 [2, 16384, 1024], P(None, 'out', 'in'), may hold values from -6 to 6
- block_table: int32 [16, 32], replicated, may hold values from 0 to 15, as said below
Outputs:
- gain: bfloat16 [16384, 1024], P('out', 'in')
Inputs may be any that keep to these rules, and one draw needn't show every extreme that they name: `block_table`: in every column the entries are 0 to 15, each once.
All inputs are finite; a program needn't handle non-finite values.
Results may differ from a plain program's by a relative error of at most 0.001.
Values may be sent and summed in bfloat16 or wider, within the bound.
A program may use at most 64 MiB of HBM per device.

v0:
```python
import jax
import jax.numpy as jnp
from jax import lax
from jax.sharding import PartitionSpec as P


def shards(kernel_weights, mode_field, diff_blocks, block_table):
    out_index = lax.axis_index("out")
    tile_rows = kernel_weights.shape[1]
    term_count = kernel_weights.shape[0]
    own_cells = diff_blocks.shape[2]
    needed_row = block_table[out_index]
    whole_field = lax.all_gather(mode_field, "out", axis=1, tiled=True)
    every_block = lax.all_gather(diff_blocks, "out", axis=1, tiled=True)
    block_count = every_block.shape[1] // tile_rows
    every_block = every_block.reshape(term_count, block_count, tile_rows, own_cells)
    arranged = jnp.take(every_block, needed_row, axis=1)
    routed = lax.all_to_all(arranged, "in", split_axis=1, concat_axis=3, tiled=True)
    spreads = [routed[term_index, 0] for term_index in range(term_count)]
    partial_value = jnp.zeros((tile_rows, whole_field.shape[1]), jnp.float32)
    for term_index in range(term_count):
        product = jnp.dot(
            kernel_weights[term_index], whole_field, preferred_element_type=jnp.float32
        )
        partial_value = partial_value + spreads[term_index].astype(jnp.float32) * product
    summed = lax.psum_scatter(partial_value, "in", scatter_dimension=1, tiled=True)
    return summed.astype(jnp.bfloat16)


def solution(mesh):
    in_specs = (P(None, "out", "in"), P("in", "out"), P(None, "out", "in"), P())
    out_specs = P("out", "in")
    return jax.shard_map(shards, mesh=mesh, in_specs=in_specs, out_specs=out_specs, check_vma=False)
```

profile of v0, /device:TPU:6, one launch (start us, length us, event | category | flops | bytes accessed | tf_op | source)
XLA Modules:
  0.0 446.2 jit_solution(17761476034946471697)
XLA Ops:
  6.5 0.0 all-gather.3.cloned.1.call-start
  6.5 0.7 all-gather.3.cloned.1.call-update
  7.3 0.7 fusion.6
  8.0 0.7 compare_and_fusion
  8.7 69.9 %all-gather.3.cloned.1.call-done = bf16[2,16384,32]{1,2,0:T(8,128)(2,1)} async-done(((bf16[2,1024,32]{1,2,0:T(8,128)(2,1)}), bf16[2,16384,32]{1,2,0:T(8,128)(2,1)}) %all-gather.3.cloned.1.call-update) | async-done | bytes 2097168 | tf_op jit(solution)/shard_map/all_gather | solution.py:14
  78.5 1.8 copy.8
  80.4 2.8 gather_fusion
  83.2 4.6 %select_bitcast_fusion = bf16[2,32,1024,32]{2,3,0,1:T(8,128)(2,1)} fusion(bf16[32,2,1024,32]{2,3,1,0:T(8,128)(2,1)} %gather_fusion, pred[32]{0:T(512)(128)(4,1)S(1)} %compare_and_fusion), kind=kLoop, calls=%fused_computation.4 | loop fusion | flops 2097152 | bytes 8388640 | tf_op jit(solution)/shard_map/jit(_take)/select_n | solution.py:17
  87.8 12.7 %all-to-all-start = ((bf16[2,32,1024,32]{2,3,0,1:T(8,128)(2,1)}), bf16[2,32,1024,32]{2,3,0,1:T(8,128)(2,1)}, u32[]{:S(2)}, u32[]{:S(2)}) async-start(bf16[2,32,1024,32]{2,3,0,1:T(8,128)(2,1)} %select_bitcast_fusion), calls=%async_computation | async-start | bytes 8388608 | tf_op jit(solution)/shard_map/all_to_all | solution.py:18
  100.5 0.0 all-gather.5.cloned.1.call-start
  100.6 0.7 all-gather.5.cloned.1.call-update
  101.3 0.0 reduce-scatter.2.cloned.1.call-start
  101.3 70.4 %all-gather.5.cloned.1.call-done = bf16[1024,1024]{0,1:T(8,128)(2,1)} async-done(((bf16[1024,64]{0,1:T(8,128)(2,1)}), bf16[1024,1024]{0,1:T(8,128)(2,1)}) %all-gather.5.cloned.1.call-update) | async-done | bytes 2097168 | tf_op jit(solution)/shard_map/all_gather | solution.py:13
  171.7 6.6 %fusion.2 = f32[1024,1024]{0,1:T(8,128)} fusion(bf16[1024,1024]{0,1:T(8,128)(2,1)} %all-gather.5.cloned.1.call-done, bf16[2,1024,1024]{2,1,0:T(8,128)(2,1)} %param.4), kind=kOutput, calls=%fused_computation.7 | convolution fusion | flops 2147483648 | bytes 8388608 | tf_op jit(solution)/shard_map/dot_general | solution.py:22
  178.3 106.0 %all-to-all-done = bf16[2,32,1024,32]{2,3,0,1:T(8,128)(2,1)} async-done(((bf16[2,32,1024,32]{2,3,0,1:T(8,128)(2,1)}), bf16[2,32,1024,32]{2,3,0,1:T(8,128)(2,1)}, u32[]{:S(2)}, u32[]{:S(2)}) %all-to-all-start) | async-done | bytes 4194336 | tf_op jit(solution)/shard_map/all_to_all | solution.py:18
  284.3 0.0 copy-start
  284.3 0.0 copy-start.1
  284.3 2.8 fusion.7
  287.1 0.6 copy-done
  287.7 0.7 copy-done.1
  288.4 6.2 %fusion = f32[1024,1024]{0,1:T(8,128)} fusion(bf16[1024,1024]{0,1:T(8,128)(2,1)S(1)} %bitcast.29, f32[1024,1024]{0,1:T(8,128)S(1)} %copy-done, bf16[1024,1024]{0,1:T(8,128)(2,1)S(1)} %bitcast.28, bf16[1024,1024]{0,1:T(8,128)(2,1)S(1)} %copy-done.1, bf16[2,1024,1024]{2,1,0:T(8,128)(2,1)} %param.4), kind=kOutput, calls=%fused_computation.2 | convolution fusion | flops 2152726528 | bytes 16777216 | tf_op jit(solution)/shard_map/dot_general | solution.py:22
  294.6 0.0 reduce-scatter.2.cloned.1.call-update
  294.6 143.5 %reduce-scatter.2.cloned.1.call-done = f32[1024,32]{0,1:T(8,128)} async-done(((f32[1024,1024]{0,1:T(8,128)}), f32[1024,32]{0,1:T(8,128)}) %reduce-scatter.2.cloned.1.call-update) | async-done | bytes 131088 | tf_op jit(solution)/shard_map/reduce_scatter | solution.py:26
  438.1 1.5 convert_element_type.19
  (1 shorter events, 0.0 us)
Async XLA Ops:
  6.5 72.0 %all-gather.3.cloned.1.call-start = ((), (), s32[]{:S(2)}) async-start(), calls=%async_computation.2 | async-start | bytes 2228224 | tf_op jit(solution)/shard_map/all_gather | solution.py:14
  87.8 196.5 %all-to-all-start = ((bf16[2,32,1024,32]{2,3,0,1:T(8,128)(2,1)}), bf16[2,32,1024,32]{2,3,0,1:T(8,128)(2,1)}, u32[]{:S(2)}, u32[]{:S(2)}) async-start(bf16[2,32,1024,32]{2,3,0,1:T(8,128)(2,1)} %select_bitcast_fusion), calls=%async_computation | async-start | bytes 8388608 | tf_op jit(solution)/shard_map/all_to_all | solution.py:18
  100.5 71.2 %all-gather.5.cloned.1.call-start = ((), (), s32[]{:S(2)}) async-start(), calls=%async_computation.3 | async-start | bytes 2228224 | tf_op jit(solution)/shard_map/all_gather | solution.py:13
  101.3 336.8 %reduce-scatter.2.cloned.1.call-start = ((), (), s32[]{:S(2)}) async-start(), calls=%async_computation.4 | async-start | bytes 4325376 | tf_op jit(solution)/shard_map/reduce_scatter | solution.py:26
  284.3 3.5 copy-start
  284.3 4.1 copy-start.1
Sparse Core Ops, SparseCore 0:
  10.7 67.8 all-gather.2
  104.6 67.0 all-gather.4
  294.7 143.3 reduce-scatter.1
where the time goes:
time: 447 us; the launch traced here: 446 us
  waiting for transfers between devices  391 us (87%)
  between operations  13.1 us (3%)
  starting transfers between devices  12.8 us (3%)
  matrix products  12.7 us (3%)
  local copies, waits for them, and re-layouts  8.73 us (2%)
  other arithmetic  7.56 us (2%)
    reduce_scatter x1, waiting for transfers between devices, shards(): lax.psum_scatter(partial_value, 'in', scatter_dimension=1, tiled=True)  143 us
    all_to_all x1, waiting for transfers between devices, shards(): lax.all_to_all(arranged, 'in', split_axis=1, concat_axis=3, tiled=True)  106 us
    all_gather x1, waiting for transfers between devices, shards(): whole_field = lax.all_gather(mode_field, 'out', axis=1, tiled=True)  70.4 us
    all_gather x1, waiting for transfers between devices, shards(): every_block = lax.all_gather(diff_blocks, 'out', axis=1, tiled=True)  69.9 us
    all_to_all x1, starting transfers between devices, shards(): lax.all_to_all(arranged, 'in', split_axis=1, concat_axis=3, tiled=True)  12.7 us
    dot_general x2, matrix products, shards(): jnp.dot(kernel_weights[term_index], whole_field, preferred_element_type=j...  12.7 us
  transfers between devices with their start and end apart: 4, of which 4 were waited for; matrix products, arithmetic and copies ran while one was open for 2% of the time, Pallas kernels for 0%

commit v1 on v0

v1 whole, which is shorter than its diff:
```python
import jax
import jax.numpy as jnp
from jax import lax
from jax.sharding import Mesh, PartitionSpec as P

PLANE = ("out", "ylo")


def shards(kernel_weights, mode_field, diff_blocks, block_table):
    terms, rows, depth = kernel_weights.shape
    own_cells = diff_blocks.shape[2]
    out_n = lax.axis_size("out")
    ylo_n = lax.axis_size("ylo")
    z_n = lax.axis_size("z")
    z_index = lax.axis_index("z")
    piece = rows // (out_n * ylo_n)
    cells = own_cells * ylo_n * z_n

    weights = lax.all_to_all(kernel_weights, PLANE, split_axis=1, concat_axis=1, tiled=True)
    weights = weights.reshape(terms, out_n, ylo_n, piece, depth)
    field = lax.all_gather(mode_field.T, PLANE, axis=0, tiled=True)
    field = field.reshape(out_n, ylo_n, cells // out_n, depth)
    blocks = lax.all_to_all(diff_blocks, PLANE, split_axis=1, concat_axis=1, tiled=True)
    blocks = lax.all_gather(blocks, "z", axis=0)
    blocks = blocks.reshape(z_n, terms, out_n, ylo_n, piece, own_cells)
    blocks = blocks.transpose(2, 1, 4, 0, 3, 5).reshape(out_n, terms, piece, cells)

    total = jnp.zeros((out_n, piece, cells), jnp.float32)
    for y in range(ylo_n):
        column = lax.dynamic_index_in_dim(block_table, z_index * ylo_n + y, 1, keepdims=False)
        chosen = jnp.take(blocks, column, axis=0, mode="clip")
        here = field[:, y].reshape(cells, depth)
        for t in range(terms):
            product = lax.dot_general(
                weights[t, :, y].reshape(out_n * piece, depth), here,
                (((1,), (1,)), ((), ())), preferred_element_type=jnp.float32)
            total = total + chosen[:, t].astype(jnp.float32) * product.reshape(out_n, piece, cells)
    summed = lax.psum_scatter(total, "z", scatter_dimension=2, tiled=True)
    summed = summed.astype(jnp.bfloat16).reshape(out_n, piece, ylo_n, own_cells)
    summed = summed.transpose(0, 2, 1, 3).reshape(out_n * ylo_n * piece, own_cells)
    return lax.all_to_all(summed, PLANE, split_axis=0, concat_axis=0, tiled=True)


def solution(mesh):
    out_n, in_n = mesh.devices.shape
    fine = Mesh(mesh.devices.reshape(out_n, in_n // 2, 2), ("out", "z", "ylo"))
    both = ("z", "ylo")
    in_specs = (P(None, "out", both), P(both, "out"), P(None, "out", both), P())
    return jax.shard_map(shards, mesh=fine, in_specs=in_specs, out_specs=P("out", both), check_vma=False)
```

time: 447 us -> 315 us (0.70)
  waiting for transfers between devices: 391 us -> 147 us
  local copies, waits for them, and re-layouts: 8.73 us -> 112 us
  blocking collectives: 0 us -> 27.2 us
  other arithmetic: 7.56 us -> 0.07 us
  matrix products: 12.7 us -> 5.59 us
  starting transfers between devices: 12.8 us -> 7.13 us
    reduce_scatter x1 -> x0, waiting for transfers between devices: 143 us -> none  [shards(): lax.psum_scatter(partial_value, 'in', scatter_dimension=1, tiled=True)]
    all_to_all x1, waiting for transfers between devices: 106 us -> 0.01 us  [shards(): lax.all_to_all(kernel_weights, PLANE, split_axis=1, concat_axis=1, tiled=...]
    unnamed x3 -> x4, waiting for transfers between devices: 1.42 us -> 76.3 us
    all_gather x2, waiting for transfers between devices: 140 us -> 70.2 us  [the longest x1 57.5 us: shards(): blocks = lax.all_gather(blocks, 'z', axis=0)]
    reshape x1 -> x3, local copies, waits for them, and re-layouts: 1.83 us -> 70.1 us  [the longest x2 48.9 us: shards(): blocks = blocks.reshape(z_n, terms, out_n, ylo_n, piece, own_cells)]
    all_to_all x0 -> x2, blocking collectives: none -> 27.2 us  [the longest x1 14.5 us: shards(): lax.all_to_all(diff_blocks, PLANE, split_axis=1, concat_axis=1, tiled=True)]
    unnamed x4 -> x18, local copies, waits for them, and re-layouts: 1.28 us -> 27.2 us
    all_to_all x0 -> x3, local copies, waits for them, and re-layouts: none -> 7.22 us  [the longest x1 5.48 us: shards(): lax.all_to_all(kernel_weights, PLANE, split_axis=1, concat_axis=1, tiled=...]
  transfers between devices with their start and end apart: 4 -> 4, of which waited for: 4 -> 3; matrix products, arithmetic and copies ran while one was open for 2% -> 28% of each run, Pallas kernels for 0% -> 0%
where the time goes in v1:
time: 315 us; the launch traced here: 311 us
  waiting for transfers between devices  147 us (47%)
  local copies, waits for them, and re-layouts  112 us (36%)
  blocking collectives  27.2 us (9%)
  between operations  13.3 us (4%)
  starting transfers between devices  7.13 us (2%)
  matrix products  5.59 us (2%)
    unnamed x4, waiting for transfers between devices  76.3 us
    all_gather x1, waiting for transfers between devices, shards(): blocks = lax.all_gather(blocks, 'z', axis=0)  57.5 us
    reshape x2, local copies, waits for them, and re-layouts, shards(): blocks = blocks.reshape(z_n, terms, out_n, ylo_n, piece, own_cells)  48.9 us
    unnamed x18, local copies, waits for them, and re-layouts  27.2 us
    reshape x1, local copies, waits for them, and re-layouts, shards(): blocks.transpose(2, 1, 4, 0, 3, 5).reshape(out_n, terms, piece, cells)  21.2 us
    all_to_all x1, blocking collectives, shards(): lax.all_to_all(diff_blocks, PLANE, split_axis=1, concat_axis=1, tiled=True)  14.5 us
    all_gather x1, waiting for transfers between devices, shards(): field = lax.all_gather(mode_field.T, PLANE, axis=0, tiled=True)  12.8 us
    all_to_all x1, blocking collectives, shards(): lax.all_to_all(summed, PLANE, split_axis=0, concat_axis=0, tiled=True)  12.7 us
  transfers between devices with their start and end apart: 4, of which 3 were waited for; matrix products, arithmetic and copies ran while one was open for 28% of the time, Pallas kernels for 0%

profile of v1, /device:TPU:6, one launch (start us, length us, event | category | flops | bytes accessed | tf_op | source)
XLA Modules:
  0.0 311.5 jit_solution(948357604762408066)
XLA Ops:
  6.5 0.0 all-gather.6.cloned.1.call-start
  6.5 1.2 copy.20
  7.7 0.5 reshape.69
  8.3 14.5 %all_to_all.22 = bf16[32,2,1024]{2,1,0:T(2,128)(2,1)S(1)} all-to-all(bf16[32,2,1024]{2,1,0:T(2,128)(2,1)S(1)} %reshape.69), channel_id=1, replica_groups=mesh['out'=16,'z'=16,'ylo'=2] {'out','ylo'}, dimensions={0} | all-to-all | bytes 262144 | tf_op jit(solution)/shard_map/all_to_all | solution.py:23
  22.8 0.3 reshape.70
  23.0 1.0 copy.21
  24.0 0.0 all-gather.6.cloned.1.call-update
  24.0 0.0 all-gather.4.cloned.1.call-start
  24.1 0.7 all-gather.4.cloned.1.call-update
  24.8 8.5 %copy.24 = bf16[2,1024,1024]{2,0,1:T(2,128)(2,1)} copy(bf16[2,1024,1024]{2,1,0:T(8,128)(2,1)} %param.4) | data formatting | bytes 8388608 | tf_op args[0]
  33.3 0.0 copy-start.3
  33.3 6.9 %all-to-all-start.1 = ((bf16[2,1024,1024]{2,0,1:T(2,128)(2,1)}), bf16[2,1024,1024]{2,0,1:T(2,128)(2,1)}, u32[]{:S(2)}, u32[]{:S(2)}) async-start(bf16[2,1024,1024]{2,0,1:T(2,128)(2,1)} %copy.24), calls=%async_computation.1 | async-start | bytes 8388608 | tf_op jit(solution)/shard_map/all_to_all | solution.py:19
  40.1 0.2 reduce-scatter.4.cloned.1.call-start
  40.4 0.0 copy-done.3
  40.4 0.2 dynamic-slice_reduce_fusion.1
  40.6 57.5 %all-gather.6.cloned.1.call-done = bf16[32,1024,32]{1,2,0:T(8,128)(2,1)} async-done(((bf16[2,1024,32]{1,2,0:T(8,128)(2,1)}), bf16[32,1024,32]{1,2,0:T(8,128)(2,1)}) %all-gather.6.cloned.1.call-update) | async-done | bytes 2097168 | tf_op jit(solution)/shard_map/all_gather | solution.py:24
  98.1 18.2 %reshape.37 = bf16[16,2,16,2,32,32]{4,3,2,5,1,0:T(2,128)(2,1)} reshape(bf16[32,1024,32]{1,2,0:T(8,128)(2,1)} %all-gather.6.cloned.1.call-done) | data formatting | bytes 4194304 | tf_op jit(solution)/shard_map/reshape | solution.py:25
  116.2 30.7 %copy.22 = bf16[16,2,16,2,32,32]{5,3,0,4,1,2:T(2,128)(2,1)} copy(bf16[16,2,16,2,32,32]{4,3,2,5,1,0:T(2,128)(2,1)} %reshape.37) | data formatting | bytes 4194304 | tf_op jit(solution)/shard_map/reshape | solution.py:25
  146.9 21.2 %reshape.38 = bf16[16,2,32,1024]{3,2,1,0:T(8,128)(2,1)S(1)} reshape(bf16[16,2,32,16,2,32]{5,4,3,2,1,0:T(2,128)(2,1)} %bitcast.75) | data formatting | bytes 4194304 | tf_op jit(solution)/shard_map/reshape | solution.py:26
  168.1 2.0 gather_fusion
  170.1 2.0 gather_fusion.1
  172.2 0.0 all-to-all-done.1
  172.2 5.5 %copy.25 = bf16[2,1024,1024]{2,1,0:T(8,128)(2,1)} copy(bf16[2,1024,1024]{2,0,1:T(2,128)(2,1)} %all-to-all-done.1) | data formatting | bytes 8388608 | tf_op jit(solution)/shard_map/all_to_all | solution.py:19
  177.6 12.8 %all-gather.4.cloned.1.call-done = bf16[2048,1024]{1,0:T(8,128)(2,1)} async-done(((bf16[64,1024]{1,0:T(8,128)(2,1)}), bf16[2048,1024]{1,0:T(8,128)(2,1)}) %all-gather.4.cloned.1.call-update) | async-done | bytes 4194320 | tf_op jit(solution)/shard_map/all_gather | solution.py:21
  190.4 0.0 copy-start
  190.4 2.9 fusion.6
  193.3 0.6 copy-done
  193.9 1.3 fusion.4
  195.2 1.3 fusion.5
  196.4 0.0 copy-start.1
  196.5 0.0 copy-start.2
  196.5 1.3 fusion.3
  197.8 0.3 copy-done.1
  198.0 0.6 copy-done.2
  198.7 1.7 fusion
  200.4 6.2 %copy.37 = f32[16,32,1024]{1,0,2:T(8,128)} copy(f32[16,32,1024]{2,1,0:T(8,128)S(1)} %fusion) | data formatting | bytes 4194304
  206.6 7.3 %reshape.65 = f32[1024,512]{1,0:T(8,128)} reshape(f32[1024,16,32]{2,1,0:T(8,128)} %bitcast.74) | data formatting | bytes 4194304
  214.0 0.0 reduce-scatter.4.cloned.1.call-update
  214.0 75.5 %reduce-scatter.4.cloned.1.call-done = f32[64,512]{1,0:T(8,128)} async-done(((f32[1024,512]{1,0:T(8,128)}), f32[64,512]{1,0:T(8,128)}) %reduce-scatter.4.cloned.1.call-update) | async-done | bytes 131088
  289.5 1.1 reshape.66
  290.6 0.3 copy.38
  290.9 0.1 fusion.7
  291.0 0.1 pad_maximum_fusion
  291.1 0.2 reshape.71
  291.3 12.7 %all_to_all.23 = bf16[32,2,512]{2,1,0:T(2,128)(2,1)S(1)} all-to-all(bf16[32,2,512]{2,1,0:T(2,128)(2,1)S(1)} %reshape.71), channel_id=1, replica_groups=mesh['out'=16,'z'=16,'ylo'=2] {'out','ylo'}, dimensions={0} | all-to-all | bytes 131072 | tf_op jit(solution)/shard_map/all_to_all | solution.py:41
  304.0 0.2 reshape.72
  304.2 0.8 copy.36
  (1 shorter events, 0.0 us)
Async XLA Ops:
  6.5 91.5 %all-gather.6.cloned.1.call-start = ((), (), s32[]{:S(2)}) async-start(), calls=%async_computation.5 | async-start | bytes 2228224 | tf_op jit(solution)/shard_map/all_gather | solution.py:24
  24.0 166.4 %all-gather.4.cloned.1.call-start = ((), (), s32[]{:S(2)}) async-start(), calls=%async_computation.4 | async-start | bytes 4325376 | tf_op jit(solution)/shard_map/all_gather | solution.py:21
  33.3 7.1 %copy-start.3 = (s32[16,32]{1,0:T(8,128)S(1)}, s32[16,32]{1,0:T(8,128)}, u32[]{:S(2)}) copy-start(s32[16,32]{1,0:T(8,128)} %param.7) | copy-start | bytes 6148
  33.3 138.9 %all-to-all-start.1 = ((bf16[2,1024,1024]{2,0,1:T(2,128)(2,1)}), bf16[2,1024,1024]{2,0,1:T(2,128)(2,1)}, u32[]{:S(2)}, u32[]{:S(2)}) async-start(bf16[2,1024,1024]{2,0,1:T(2,128)(2,1)} %copy.24), calls=%async_computation.1 | async-start | bytes 8388608 | tf_op jit(solution)/shard_map/all_to_all | solution.py:19
  40.1 249.4 %reduce-scatter.4.cloned.1.call-start = ((), (), s32[]{:S(2)}) async-start(), calls=%async_computation.6 | async-start | bytes 2228224
  190.4 3.5 %copy-start = (bf16[2,1024,1024]{2,1,0:T(8,128)(2,1)S(1)}, bf16[2,1024,1024]{2,1,0:T(8,128)(2,1)}, u32[]{:S(2)}) copy-start(bf16[2,1024,1024]{2,1,0:T(8,128)(2,1)} %copy.25) | copy-start | bytes 12582916
  196.4 1.6 copy-start.1
  196.5 2.2 copy-start.2
Sparse Core Ops, SparseCore 0:
  24.2 73.8 all-gather.5
  100.2 90.2 all-gather.3
  214.1 75.3 reduce-scatter.3

commit v2 on v0

v2 whole, which is shorter than its diff:
```python
import jax
import jax.numpy as jnp
from jax import lax
from jax.experimental import pallas as pl
from jax.experimental.pallas import tpu as pltpu
from jax.sharding import PartitionSpec as P

MESH = pl.DeviceIdType.MESH
BF16, F32, I32 = jnp.bfloat16, jnp.float32, jnp.int32

NP, NZ, NR = 4, 16, 16
TERMS, ROWS, DEPTH, CELLS = 2, 1024, 1024, 1024
PIECE, HALF = 32, 16
OWN = 32
FIELD = 64
CHUNK = 64
LANES = NR * HALF

OFFSETS = (1, 3, 2)
FAR = ((2, 2), (2, 1), (1, 2), (2, 3), (3, 2), (2, 0), (0, 2), (1, 1), (3, 3), (1, 3), (3, 1), (1, 0), (0, 1), (3, 0), (0, 3))
PEERS = tuple((dx, dy, dc) for dc in (0, 1) for dx, dy in FAR) + ((0, 0, 1),)
EARLY = 10


def rem(a, n):
    return lax.rem(a, jnp.int32(n))


def hot(shape, rule):
    rows = lax.broadcasted_iota(I32, shape, 0)
    lanes = lax.broadcasted_iota(I32, shape, 1)
    return jnp.where(rule(rows, lanes), 1.0, 0.0).astype(BF16)


def dot(a, b):
    return jnp.dot(a, b, preferred_element_type=F32)


def dot_nt(a, b):
    return lax.dot_general(a, b, (((1,), (1,)), ((), ())), preferred_element_type=F32)


def kernel(table, w_hbm, m_hbm, d_ref, out_ref,
           weights, field, packed, packets, blocks, spread, pick, unpack, results, finals, give_r, give_l, take_r, take_l, sums,
           own_sem, d_send, d_recv, m_send, m_recv, w_send, w_recv, b_send, b_recv, r_send, r_recv, l_send, l_recv, f_send, f_recv):
    o, i = lax.axis_index("out"), lax.axis_index("in")
    x, y_hi, core = o // 4, rem(o // 2, 2), rem(o, 2)
    z, y_lo = i // 2, rem(i, 2)
    y = y_hi * 2 + y_lo
    me = o * 2 + y_lo

    def place(dx, dy, dc=0, dz=0):
        px, py, pc, pz = rem(x + dx, NP), rem(y + dy, NP), rem(core + dc, 2), rem(z + dz, NZ)
        return px * 4 + (py // 2) * 2 + pc, pz * 2 + rem(py, 2)

    def piece_of(device):
        return device[0] * 2 + rem(device[1], 2)

    def remote(src, dst, send, recv, device):
        return pltpu.make_async_remote_copy(src, dst, send, recv, device_id=device, device_id_type=MESH)

    up, down = place(0, 0, 0, 1), place(0, 0, 0, NZ - 1)
    devices = [place(*p) for p in PEERS]
    sources = [place(NP - p[0], NP - p[1], p[2]) for p in PEERS]
    sends = []

    def packing(rows, lanes):
        return (rows // 128 == rem(lanes, 128) // 32) & (rem(rows, 128) == (lanes // 128) * 32 + rem(lanes, 32))

    wide = hot((512, 512), packing)
    flat = d_ref[...].reshape(TERMS * OWN, ROWS)
    stacked = jnp.concatenate(
        [jnp.concatenate([flat[b * 16:(b + 1) * 16, t * 128:(t + 1) * 128] for b in range(4)], axis=1) for t in range(8)], axis=0)
    packed[...] = dot(stacked, wide).astype(BF16).reshape(8, 16, 512)

    barrier = pltpu.get_barrier_semaphore()
    for device in devices + [up, down]:
        pl.semaphore_signal(barrier, inc=1, device_id=device, device_id_type=MESH)
    pl.semaphore_wait(barrier, len(devices) + 2)

    def packet(piece):
        return packed.at[piece // 4, :, pl.ds(pl.multiple_of(rem(piece, 4) * 128, 128), 128)]

    def packet_slot(device):
        return packets.at[rem(device[1], 2), :, pl.ds(pl.multiple_of(device[0] * 128, 128), 128)]

    def run(copy):
        copy.start()
        sends.append(copy)

    for n, device in enumerate(devices):
        run(remote(packet(piece_of(device)), packet_slot((o, i)), d_send.at[n], d_recv.at[n], device))
    own_packet = pltpu.make_async_copy(packet(me), packet_slot((o, i)), own_sem.at[0])
    own_packet.start()

    def along(a, b):
        return a * (1 - core) + b * core, b * (1 - core) + a * core

    def shard(dx, dy, dc=0):
        device = place(dx, dy, dc)
        return field.at[rem(device[1], 2), pl.ds(pl.multiple_of(device[0] * FIELD, FIELD), FIELD), :]

    partner = place(0, 0, 1)
    own_field = pltpu.make_async_copy(m_hbm, shard(0, 0), own_sem.at[1])
    own_field.start()
    for n, a in enumerate(OFFSETS):
        run(remote(m_hbm, shard(0, 0), m_send.at[n], m_recv.at[n], place(*along(a, 0))))
    for n, a in enumerate(OFFSETS):
        run(remote(m_hbm, shard(0, 0), m_send.at[3 + n], m_recv.at[3 + n], place(*along(0, a))))
    run(remote(m_hbm, shard(0, 0), m_send.at[15], m_recv.at[15], partner))

    def slab(half, device):
        return weights.at[half, rem(device[1], 2), :, pl.ds(pl.multiple_of(device[0] * HALF, HALF), HALF), :]

    def rows_for(half, piece):
        return w_hbm.at[:, pl.ds(pl.multiple_of(piece * PIECE + half * HALF, HALF), HALF), :]

    def send_weights(half, first, last):
        for n in range(first, last):
            run(remote(rows_for(half, piece_of(devices[n])), slab(half, (o, i)), w_send.at[half, n], w_recv.at[half, n], devices[n]))

    own_weights = [pltpu.make_async_copy(rows_for(half, me), slab(half, (o, i)), own_sem.at[2 + half]) for half in range(2)]
    for copy in own_weights:
        copy.start()
    send_weights(0, 0, EARLY)

    def unpacking(rows, lanes):
        return (rem(lanes, 128) // 16 == rows // 128) & (rem(rows, 128) == (lanes // 128) * 16 + rem(lanes, 16))

    spread[...] = hot((1024, 1024), unpacking)

    own_packet.wait()
    for n, source in enumerate(sources):
        remote(packet(me), packet_slot(source), d_send.at[n], d_recv.at[n], source).wait_recv()
    for q in range(2):
        opened = dot(packets[...].reshape(32, 2048)[:, q * 1024:(q + 1) * 1024], spread[...]).astype(BF16)
        for b in range(4):
            for half in range(2):
                for s in range(2):
                    row = (b // 2) * 64 + s * 32 + (b % 2) * 16
                    lane = (b * 2 + half) * 128
                    blocks[z, half, row:row + 16, q * 128:(q + 1) * 128] = opened[s * 16:(s + 1) * 16, lane:lane + 128]

    def ring_send(k):
        for half in range(2):
            if k < 8:
                at = blocks.at[rem(z - k + NZ, NZ), half]
                run(remote(at, at, b_send.at[0, half, k], b_recv.at[0, half, k], up))
            if k < 7:
                at = blocks.at[rem(z + k, NZ), half]
                run(remote(at, at, b_send.at[1, half, k], b_recv.at[1, half, k], down))

    def ring_wait(k):
        for half in range(2):
            if k < 8:
                at = blocks.at[rem(z - k - 1 + NZ, NZ), half]
                remote(at, at, b_send.at[0, half, k], b_recv.at[0, half, k], down).wait_recv()
            if k < 7:
                at = blocks.at[rem(z + k + 1, NZ), half]
                remote(at, at, b_send.at[1, half, k], b_recv.at[1, half, k], up).wait_recv()

    ring_send(0)

    own_field.wait()
    for m, a in enumerate(OFFSETS):
        here = shard(*along(NP - a, 0))
        remote(here, here, m_send.at[m], m_recv.at[m], place(*along(a, 0))).wait_recv()
        for n, b in enumerate(OFFSETS):
            slot = 6 + m * 3 + n
            run(remote(here, here, m_send.at[slot], m_recv.at[slot], place(*along(0, b))))
        run(remote(here, here, m_send.at[16 + m], m_recv.at[16 + m], partner))

    send_weights(0, EARLY, len(PEERS))
    send_weights(1, 0, len(PEERS))

    def forward_field(m, n):
        a = 0 if m == 0 else NP - OFFSETS[m - 1]
        slot = 3 + m * 3 + n
        here = shard(*along(a, NP - OFFSETS[n]))
        remote(here, here, m_send.at[slot], m_recv.at[slot], place(*along(0, OFFSETS[n]))).wait_recv()
        back = 19 + m * 3 + n
        run(remote(here, here, m_send.at[back], m_recv.at[back], partner))

    ring_wait(0)
    ring_send(1)
    for n in range(3):
        forward_field(0, n)
    ring_wait(1)
    ring_send(2)
    for m in range(1, 4):
        for n in range(3):
            forward_field(m, n)

    for s in range(2):
        lanes = lax.broadcasted_iota(I32, (1, LANES), 1)
        wanted = jnp.zeros((1, LANES), I32)
        for r in range(NR):
            wanted = jnp.where(lanes // HALF == r, table[r, z * 2 + s], wanted)
        pick[s] = hot((LANES, LANES), lambda rows, cols: (rows // HALF == wanted) & (rem(rows, HALF) == rem(cols, HALF)))

    def closing(rows, lanes):
        inner = rem(lanes, 128)
        return (inner // 16 == rows // 128) & (rem(rows, 128) == (lanes // 128) * 16 + rem(lanes, 16))

    spread[0:512, :] = hot((512, 1024), closing)
    for b in range(2):
        unpack[b] = hot((512, 128), lambda rows, lanes: (rows // 128 == lanes // 32) & (rem(rows, 128) == b * 32 + rem(lanes, 32)))

    for k in range(2, 7):
        ring_wait(k)
        ring_send(k + 1)
    ring_wait(7)

    for n in range(16):
        if n == 0:
            here = shard(0, 0, 1)
        elif n < 4:
            a = NP - OFFSETS[n - 1]
            here = shard(a * core, a * (1 - core), 1)
        else:
            m, q = (n - 4) // 3, (n - 4) % 3
            a = 0 if m == 0 else NP - OFFSETS[m - 1]
            b = NP - OFFSETS[q]
            here = shard(a * core + b * (1 - core), b * core + a * (1 - core), 1)
        remote(here, here, m_send.at[15 + n], m_recv.at[15 + n], partner).wait_recv()

    def chunk_pair(half, first, second):
        total = None
        for s in range(2):
            cells = jnp.concatenate(
                [field[s, pl.ds(pl.multiple_of(first * CHUNK, CHUNK), CHUNK), :],
                 field[s, pl.ds(pl.multiple_of(second * CHUNK, CHUNK), CHUNK), :]], axis=0)
            product = dot_nt(cells, weights[half, s].reshape(TERMS * LANES, DEPTH))
            chosen = dot(jnp.concatenate([blocks[first, half], blocks[second, half]], axis=0), pick[s])
            for t in range(TERMS):
                scale = jnp.concatenate([chosen[t * 64:t * 64 + 64], chosen[128 + t * 64:192 + t * 64]], axis=0)
                part = scale * product[:, t * LANES:(t + 1) * LANES]
                total = part if total is None else total + part
        return total

    def right(half, k, sub):
        return remote(give_r.at[half, k, sub], take_r.at[half, k, sub], r_send.at[half, k, sub], r_recv.at[half, k, sub], up)

    def left(half, k, sub):
        return remote(give_l.at[half, k, sub], take_l.at[half, k, sub], l_send.at[half, k, sub], l_recv.at[half, k, sub], down)

    for half in range(2):
        own_weights[half].wait()
        for n, source in enumerate(sources):
            remote(rows_for(half, me), slab(half, source), w_send.at[half, n], w_recv.at[half, n], source).wait_recv()

        total = chunk_pair(half, rem(z + 8, NZ), rem(z + 9, NZ))
        for sub in range(2):
            give_r[half, 0, sub] = total[:CHUNK, sub * 128:(sub + 1) * 128]
            right(half, 0, sub).start()
            give_l[half, 0, sub] = total[CHUNK:, sub * 128:(sub + 1) * 128]
            left(half, 0, sub).start()

        def ring_step(k, carry, half=half):
            total = chunk_pair(half, rem(z + 8 - k + NZ, NZ), rem(z + 9 + k, NZ))
            for sub in range(2):
                right(half, k - 1, sub).wait_recv()
                give_r[half, k, sub] = total[:CHUNK, sub * 128:(sub + 1) * 128] + take_r[half, k - 1, sub]
                right(half, k, sub).start()
                left(half, k - 1, sub).wait_recv()
                give_l[half, k, sub] = total[CHUNK:, sub * 128:(sub + 1) * 128] + take_l[half, k - 1, sub]

                @pl.when(k < 7)
                def _():
                    left(half, k, sub).start()
            return carry

        lax.fori_loop(1, 8, ring_step, jnp.int32(0))

    for half in range(2):
        for sub in range(2):
            right(half, 7, sub).wait_recv()
            sums[half * 2 + sub] = (give_l[half, 7, sub] + take_r[half, 7, sub]).astype(BF16)

    closed = jnp.concatenate(
        [jnp.concatenate([sums[half * 2 + q, s * 32 + b * 16:s * 32 + b * 16 + 16, :] for b in range(2) for half in range(2)], axis=1)
         for s in range(2) for q in range(2)], axis=0)
    results[...] = dot(closed, spread[0:512, :]).astype(BF16).reshape(2, 2, 16, 1024)

    def result_for(device):
        return results.at[rem(device[1], 2), device[0] // 8, :, pl.ds(pl.multiple_of(rem(device[0], 8) * 128, 128), 128)]

    def result_slot(piece):
        return finals.at[piece // 4, :, pl.ds(pl.multiple_of(rem(piece, 4) * 128, 128), 128)]

    for n, device in enumerate(devices):
        run(remote(result_for(device), result_slot(me), f_send.at[n], f_recv.at[n], device))
    own_result = pltpu.make_async_copy(result_for((o, i)), result_slot(me), own_sem.at[4])
    own_result.start()

    for copy in sends[:-len(devices)]:
        copy.wait_send()
    for half in range(2):
        for sub in range(2):
            for k in range(8):
                right(half, k, sub).wait_send()
                if k < 7:
                    left(half, k, sub).wait_send()

    own_result.wait()
    for n, source in enumerate(sources):
        remote(result_for(source), result_slot(piece_of(source)), f_send.at[n], f_recv.at[n], source).wait_recv()
    for b in range(2):
        opened = dot(finals[...].reshape(128, 512), unpack[b]).astype(BF16)
        for j in range(8):
            out_ref[b * 16:(b + 1) * 16, j * 128:(j + 1) * 128] = opened[j * 16:(j + 1) * 16, :]
    for copy in sends[-len(devices):]:
        copy.wait_send()


def shards(kernel_weights, mode_field, diff_blocks, block_table):
    peers = len(PEERS)
    dma = pltpu.SemaphoreType.DMA
    vmem = pl.BlockSpec(memory_space=pltpu.VMEM)
    gain = pl.pallas_call(
        kernel,
        out_shape=jax.ShapeDtypeStruct((OWN, ROWS), BF16),
        in_specs=[pl.BlockSpec(memory_space=pltpu.SMEM), pl.BlockSpec(memory_space=pl.ANY),
                  pl.BlockSpec(memory_space=pl.ANY), vmem],
        out_specs=vmem,
        scratch_shapes=[
            pltpu.VMEM((2, 2, TERMS, LANES, DEPTH), BF16),
            pltpu.VMEM((2, CELLS, DEPTH), BF16),
            pltpu.VMEM((8, 16, 512), BF16),
            pltpu.VMEM((2, 16, 2048), BF16),
            pltpu.VMEM((NZ, 2, TERMS * CHUNK, LANES), BF16),
            pltpu.VMEM((1024, 1024), BF16),
            pltpu.VMEM((2, LANES, LANES), BF16),
            pltpu.VMEM((2, 512, 128), BF16),
            pltpu.VMEM((2, 2, 16, 1024), BF16),
            pltpu.VMEM((8, 16, 512), BF16),
            pltpu.VMEM((2, 8, 2, CHUNK, 128), F32),
            pltpu.VMEM((2, 8, 2, CHUNK, 128), F32),
            pltpu.VMEM((2, 8, 2, CHUNK, 128), F32),
            pltpu.VMEM((2, 8, 2, CHUNK, 128), F32),
            pltpu.VMEM((4, CHUNK, 128), BF16),
            dma((5,)),
            dma((peers,)), dma((peers,)),
            dma((31,)), dma((31,)),
            dma((2, peers)), dma((2, peers)),
            dma((2, 2, 8)), dma((2, 2, 8)),
            dma((2, 8, 2)), dma((2, 8, 2)),
            dma((2, 8, 2)), dma((2, 8, 2)),
            dma((peers,)), dma((peers,)),
        ],
        compiler_params=pltpu.CompilerParams(collective_id=0, has_side_effects=True, vmem_limit_bytes=48 * 2**20),
        name="collision_gain",
    )(block_table, kernel_weights, mode_field.T, diff_blocks.transpose(0, 2, 1))
    return gain.T


def solution(mesh):
    in_specs = (P(None, "out", "in"), P("in", "out"), P(None, "out", "in"), P())
    return jax.shard_map(shards, mesh=mesh, in_specs=in_specs, out_specs=P("out", "in"), check_vma=False)
```

time: 447 us -> 153 us (0.34)
  waiting for transfers between devices: 391 us -> 0 us
  Pallas kernels: 0 us -> 147 us
  between operations: 13.1 us -> 0.01 us
  starting transfers between devices: 12.8 us -> 0 us
  matrix products: 12.7 us -> 0 us
  other arithmetic: 7.56 us -> 0 us
    pallas_call x0 -> x1, Pallas kernels: none -> 147 us  [shards(): pl.pallas_call(kernel, out_shape=jax.ShapeDtypeStruct((OWN, ROWS), BF16),...]
    reduce_scatter x1 -> x0, waiting for transfers between devices: 143 us -> none  [shards(): lax.psum_scatter(partial_value, 'in', scatter_dimension=1, tiled=True)]
    all_gather x2 -> x0, waiting for transfers between devices: 140 us -> none  [the longest x1 70.4 us: shards(): whole_field = lax.all_gather(mode_field, 'out', axis=1, tiled=True)]
    all_to_all x1 -> x0, waiting for transfers between devices: 106 us -> none  [shards(): lax.all_to_all(arranged, 'in', split_axis=1, concat_axis=3, tiled=True)]
    all_to_all x1 -> x0, starting transfers between devices: 12.7 us -> none  [shards(): lax.all_to_all(arranged, 'in', split_axis=1, concat_axis=3, tiled=True)]
    dot_general x2 -> x0, matrix products: 12.7 us -> none  [shards(): jnp.dot(kernel_weights[term_index], whole_field, preferred_element_type=j...]
    select_n x2 -> x0, other arithmetic: 5.31 us -> none  [shards(): arranged = jnp.take(every_block, needed_row, axis=1)]
  transfers between devices with their start and end apart: 4 -> 0, of which waited for: 4 -> 0; matrix products, arithmetic and copies ran while one was open for 2% -> 0% of each run, Pallas kernels for 0% -> 0%
where the time goes in v2:
time: 153 us; the launch traced here: 152 us
  Pallas kernels  147 us (96%)
  local copies, waits for them, and re-layouts  5.32 us (3%)
    pallas_call x1, Pallas kernels, shards(): pl.pallas_call(kernel, out_shape=jax.ShapeDtypeStruct((OWN, ROWS), BF16),...  147 us
    unnamed x9, local copies, waits for them, and re-layouts  5.32 us

profile of v2, /device:TPU:6, one launch (start us, length us, event | category | flops | bytes accessed | tf_op | source)
XLA Modules:
  0.0 152.1 jit_solution(6971266240616909780)
XLA Ops:
  0.0 0.0 copy-start
  0.0 2.2 %copy-done = bf16[2,1024,1024]{2,1,0:T(8,128)(2,1)S(1)} copy-done((bf16[2,1024,1024]{2,1,0:T(8,128)(2,1)S(1)}, bf16[2,1024,1024]{2,1,0:T(8,128)(2,1)}, u32[]{:S(2)}) %copy-start) | copy-done | bytes 4194328
  2.2 0.0 copy-start.1
  2.2 0.9 copy-done.1
  3.1 0.0 copy-start.2
  3.1 0.9 copy-done.2
  4.0 0.0 copy-start.3
  4.0 0.7 copy-done.3
  4.7 146.7 %collision_gain.1 = bf16[32,1024]{1,0:T(8,128)(2,1)S(1)} custom-call(s32[16,32]{1,0:T(8,128)S(1)} %copy-done.3, bf16[2,1024,1024]{2,1,0:T(8,128)(2,1)S(1)} %copy-done, bf16[64,1024]{1,0:T(8,128)(2,1)S(1)} %bitcast.4, bf16[2,32,1024]{2,1,0:T(8,128)(2,1)S(1)} %bitcast.5), custom_call_target="tpu_custom_call" | custom-call | tf_op jit(solution)/shard_map/collision_gain/pallas_call | solution.py:320
  151.4 0.6 copy.6
Async XLA Ops:
  0.0 2.2 %copy-start = (bf16[2,1024,1024]{2,1,0:T(8,128)(2,1)S(1)}, bf16[2,1024,1024]{2,1,0:T(8,128)(2,1)}, u32[]{:S(2)}) copy-start(bf16[2,1024,1024]{2,1,0:T(8,128)(2,1)} %w_hbm.1) | copy-start | bytes 12582916
  2.2 0.9 copy-start.1
  3.1 0.9 copy-start.2
  4.0 0.7 copy-start.3

commit v3 on v2

--- a/solution.py
+++ b/solution.py
@@ -19,7 +19,7 @@
 OFFSETS = (1, 3, 2)
 FAR = ((2, 2), (2, 1), (1, 2), (2, 3), (3, 2), (2, 0), (0, 2), (1, 1), (3, 3), (1, 3), (3, 1), (1, 0), (0, 1), (3, 0), (0, 3))
 PEERS = tuple((dx, dy, dc) for dc in (0, 1) for dx, dy in FAR) + ((0, 0, 1),)
-EARLY = 10
+EARLY = 12
 
 
 def rem(a, n):
@@ -60,6 +60,7 @@
         return pltpu.make_async_remote_copy(src, dst, send, recv, device_id=device, device_id_type=MESH)
 
     up, down = place(0, 0, 0, 1), place(0, 0, 0, NZ - 1)
+    up_two, down_two = place(0, 0, 0, 2), place(0, 0, 0, NZ - 2)
     devices = [place(*p) for p in PEERS]
     sources = [place(NP - p[0], NP - p[1], p[2]) for p in PEERS]
     sends = []
@@ -74,9 +75,9 @@
     packed[...] = dot(stacked, wide).astype(BF16).reshape(8, 16, 512)
 
     barrier = pltpu.get_barrier_semaphore()
-    for device in devices + [up, down]:
+    for device in devices + [up, down, up_two, down_two]:
         pl.semaphore_signal(barrier, inc=1, device_id=device, device_id_type=MESH)
-    pl.semaphore_wait(barrier, len(devices) + 2)
+    pl.semaphore_wait(barrier, len(devices) + 4)
 
     def packet(piece):
         return packed.at[piece // 4, :, pl.ds(pl.multiple_of(rem(piece, 4) * 128, 128), 128)]
@@ -119,9 +120,8 @@
         for n in range(first, last):
             run(remote(rows_for(half, piece_of(devices[n])), slab(half, (o, i)), w_send.at[half, n], w_recv.at[half, n], devices[n]))
 
-    own_weights = [pltpu.make_async_copy(rows_for(half, me), slab(half, (o, i)), own_sem.at[2 + half]) for half in range(2)]
-    for copy in own_weights:
-        copy.start()
+    for half in range(2):
+        pltpu.make_async_copy(rows_for(half, me), slab(half, (o, i)), own_sem.at[2 + half]).start()
     send_weights(0, 0, EARLY)
 
     def unpacking(rows, lanes):
@@ -142,22 +142,26 @@
                     blocks[z, half, row:row + 16, q * 128:(q + 1) * 128] = opened[s * 16:(s + 1) * 16, lane:lane + 128]
 
     def ring_send(k):
-        for half in range(2):
+        for sub in range(4):
+            lot = pl.ds(sub % 2 * 64, 64)
             if k < 8:
-                at = blocks.at[rem(z - k + NZ, NZ), half]
-                run(remote(at, at, b_send.at[0, half, k], b_recv.at[0, half, k], up))
+                at = blocks.at[rem(z - k + NZ, NZ), sub // 2, lot]
+                run(remote(at, at, b_send.at[0, sub, k], b_recv.at[0, sub, k], up))
             if k < 7:
-                at = blocks.at[rem(z + k, NZ), half]
-                run(remote(at, at, b_send.at[1, half, k], b_recv.at[1, half, k], down))
-
-    def ring_wait(k):
-        for half in range(2):
-            if k < 8:
-                at = blocks.at[rem(z - k - 1 + NZ, NZ), half]
-                remote(at, at, b_send.at[0, half, k], b_recv.at[0, half, k], down).wait_recv()
+                at = blocks.at[rem(z + k, NZ), sub // 2, lot]
+                run(remote(at, at, b_send.at[1, sub, k], b_recv.at[1, sub, k], down))
+
+    def ring_pass(k):
+        for sub in range(4):
+            lot = pl.ds(sub % 2 * 64, 64)
+            at = blocks.at[rem(z - k - 1 + NZ, NZ), sub // 2, lot]
+            remote(at, at, b_send.at[0, sub, k], b_recv.at[0, sub, k], down).wait_recv()
             if k < 7:
-                at = blocks.at[rem(z + k + 1, NZ), half]
-                remote(at, at, b_send.at[1, half, k], b_recv.at[1, half, k], up).wait_recv()
+                run(remote(at, at, b_send.at[0, sub, k + 1], b_recv.at[0, sub, k + 1], up))
+                at = blocks.at[rem(z + k + 1, NZ), sub // 2, lot]
+                remote(at, at, b_send.at[1, sub, k], b_recv.at[1, sub, k], up).wait_recv()
+                if k < 6:
+                    run(remote(at, at, b_send.at[1, sub, k + 1], b_recv.at[1, sub, k + 1], down))
 
     ring_send(0)
 
@@ -181,15 +185,8 @@
         back = 19 + m * 3 + n
         run(remote(here, here, m_send.at[back], m_recv.at[back], partner))
 
-    ring_wait(0)
-    ring_send(1)
-    for n in range(3):
-        forward_field(0, n)
-    ring_wait(1)
-    ring_send(2)
-    for m in range(1, 4):
-        for n in range(3):
-            forward_field(m, n)
+    ring_pass(0)
+    ring_pass(1)
 
     for s in range(2):
         lanes = lax.broadcasted_iota(I32, (1, LANES), 1)
@@ -206,10 +203,16 @@
     for b in range(2):
         unpack[b] = hot((512, 128), lambda rows, lanes: (rows // 128 == lanes // 32) & (rem(rows, 128) == b * 32 + rem(lanes, 32)))
 
-    for k in range(2, 7):
-        ring_wait(k)
-        ring_send(k + 1)
-    ring_wait(7)
+    ring_pass(2)
+    ring_pass(3)
+    for n in range(3):
+        forward_field(0, n)
+    ring_pass(4)
+    for m in range(1, 4):
+        for n in range(3):
+            forward_field(m, n)
+    for k in range(5, 8):
+        ring_pass(k)
 
     for n in range(16):
         if n == 0:
@@ -239,43 +242,47 @@
         return total
 
     def right(half, k, sub):
-        return remote(give_r.at[half, k, sub], take_r.at[half, k, sub], r_send.at[half, k, sub], r_recv.at[half, k, sub], up)
+        target = up_two if k in (1, 3, 5) else up
+        return remote(give_r.at[half, k, sub], take_r.at[half, k, sub], r_send.at[half, k, sub], r_recv.at[half, k, sub], target)
 
     def left(half, k, sub):
-        return remote(give_l.at[half, k, sub], take_l.at[half, k, sub], l_send.at[half, k, sub], l_recv.at[half, k, sub], down)
-
-    for half in range(2):
-        own_weights[half].wait()
+        target = down_two if k in (0, 2, 4) else down
+        return remote(give_l.at[half, k, sub], take_l.at[half, k, sub], l_send.at[half, k, sub], l_recv.at[half, k, sub], target)
+
+    def reduce_half(half, carry):
+        pltpu.make_async_copy(rows_for(half, me), slab(half, (o, i)), own_sem.at[2 + half]).wait()
         for n, source in enumerate(sources):
             remote(rows_for(half, me), slab(half, source), w_send.at[half, n], w_recv.at[half, n], source).wait_recv()
-
-        total = chunk_pair(half, rem(z + 8, NZ), rem(z + 9, NZ))
-        for sub in range(2):
-            give_r[half, 0, sub] = total[:CHUNK, sub * 128:(sub + 1) * 128]
-            right(half, 0, sub).start()
-            give_l[half, 0, sub] = total[CHUNK:, sub * 128:(sub + 1) * 128]
-            left(half, 0, sub).start()
-
-        def ring_step(k, carry, half=half):
+        for k in range(8):
             total = chunk_pair(half, rem(z + 8 - k + NZ, NZ), rem(z + 9 + k, NZ))
+            raw, chain = (right, left) if k % 2 == 0 else (left, right)
+            give, take = (give_l, take_l) if k % 2 == 0 else (give_r, take_r)
+            other = give_r if k % 2 == 0 else give_l
+            raw_rows, chain_rows = (total[:CHUNK], total[CHUNK:]) if k % 2 == 0 else (total[CHUNK:], total[:CHUNK])
             for sub in range(2):
-                right(half, k - 1, sub).wait_recv()
-                give_r[half, k, sub] = total[:CHUNK, sub * 128:(sub + 1) * 128] + take_r[half, k - 1, sub]
-                right(half, k, sub).start()
-                left(half, k - 1, sub).wait_recv()
-                give_l[half, k, sub] = total[CHUNK:, sub * 128:(sub + 1) * 128] + take_l[half, k - 1, sub]
-
-                @pl.when(k < 7)
-                def _():
-                    left(half, k, sub).start()
-            return carry
-
-        lax.fori_loop(1, 8, ring_step, jnp.int32(0))
+                other[half, k, sub] = raw_rows[:, sub * 128:(sub + 1) * 128]
+                if k < 7:
+                    raw(half, k, sub).start()
+            for sub in range(2):
+                value = chain_rows[:, sub * 128:(sub + 1) * 128]
+                if k >= 1:
+                    chain(half, k - 1, sub).wait_recv()
+                    value = value + take[half, k - 1, sub]
+                if k >= 2 and k - 2 >= k % 2:
+                    chain(half, k - 2, sub).wait_recv()
+                    value = value + take[half, k - 2, sub]
+                give[half, k, sub] = value
+                chain(half, k, sub).start()
+        return carry
+
+    lax.fori_loop(0, 2, reduce_half, jnp.int32(0))
 
     for half in range(2):
         for sub in range(2):
+            left(half, 6, sub).wait_recv()
             right(half, 7, sub).wait_recv()
-            sums[half * 2 + sub] = (give_l[half, 7, sub] + take_r[half, 7, sub]).astype(BF16)
+            total = give_l[half, 7, sub] + take_l[half, 6, sub] + take_r[half, 7, sub]
+            sums[half * 2 + sub] = total.astype(BF16)
 
     closed = jnp.concatenate(
         [jnp.concatenate([sums[half * 2 + q, s * 32 + b * 16:s * 32 + b * 16 + 16, :] for b in range(2) for half in range(2)], axis=1)
@@ -343,12 +350,12 @@
             dma((peers,)), dma((peers,)),
             dma((31,)), dma((31,)),
             dma((2, peers)), dma((2, peers)),
-            dma((2, 2, 8)), dma((2, 2, 8)),
+            dma((2, 4, 8)), dma((2, 4, 8)),
             dma((2, 8, 2)), dma((2, 8, 2)),
             dma((2, 8, 2)), dma((2, 8, 2)),
             dma((peers,)), dma((peers,)),
         ],
-        compiler_params=pltpu.CompilerParams(collective_id=0, has_side_effects=True, vmem_limit_bytes=48 * 2**20),
+        compiler_params=pltpu.CompilerParams(collective_id=0, has_side_effects=True, vmem_limit_bytes=63 * 2**20),
         name="collision_gain",
     )(block_table, kernel_weights, mode_field.T, diff_blocks.transpose(0, 2, 1))
     return gain.T

time: 153 us -> 127 us (0.83)
  Pallas kernels: 147 us -> 123 us
  local copies, waits for them, and re-layouts: 5.32 us -> 1.47 us
    pallas_call x1, Pallas kernels: 147 us -> 123 us  [shards(): pl.pallas_call(kernel, out_shape=jax.ShapeDtypeStruct((OWN, ROWS), BF16),...]
    unnamed x9 -> x1, local copies, waits for them, and re-layouts: 5.32 us -> 1.47 us
where the time goes in v3:
time: 127 us; the launch traced here: 125 us
  Pallas kernels  123 us (97%)
  local copies, waits for them, and re-layouts  1.47 us (1%)
    pallas_call x1, Pallas kernels, shards(): pl.pallas_call(kernel, out_shape=jax.ShapeDtypeStruct((OWN, ROWS), BF16),...  123 us

profile of v3, /device:TPU:6, one launch (start us, length us, event | category | flops | bytes accessed | tf_op | source)
XLA Modules:
  0.0 124.9 jit_solution(6092090998584935887)
XLA Ops:
  0.0 123.4 %collision_gain.1 = bf16[32,1024]{1,0:T(8,128)(2,1)} custom-call(s32[16,32]{1,0:T(8,128)} %table.1, bf16[2,1024,1024]{2,1,0:T(8,128)(2,1)} %w_hbm.1, bf16[64,1024]{1,0:T(8,128)(2,1)} %bitcast.4, bf16[2,32,1024]{2,1,0:T(8,128)(2,1)} %bitcast.5), custom_call_target="tpu_custom_call" | custom-call | tf_op jit(solution)/shard_map/collision_gain/pallas_call | solution.py:327
  123.5 1.5 %copy.6 = bf16[1024,32]{0,1:T(8,128)(2,1)} copy(bf16[1024,32]{0,1:T(8,128)(2,1)} %bitcast.3) | data formatting | bytes 131072

commit v4 on v3

--- a/solution.py
+++ b/solution.py
@@ -227,19 +227,19 @@
             here = shard(a * core + b * (1 - core), b * core + a * (1 - core), 1)
         remote(here, here, m_send.at[15 + n], m_recv.at[15 + n], partner).wait_recv()
 
-    def chunk_pair(half, first, second):
-        total = None
+    def chunk_terms(half, chunks):
+        n = len(chunks)
+        totals = [None] * n
         for s in range(2):
-            cells = jnp.concatenate(
-                [field[s, pl.ds(pl.multiple_of(first * CHUNK, CHUNK), CHUNK), :],
-                 field[s, pl.ds(pl.multiple_of(second * CHUNK, CHUNK), CHUNK), :]], axis=0)
+            cells = jnp.concatenate([field[s, pl.ds(pl.multiple_of(c * CHUNK, CHUNK), CHUNK), :] for c in chunks], axis=0)
             product = dot_nt(cells, weights[half, s].reshape(TERMS * LANES, DEPTH))
-            chosen = dot(jnp.concatenate([blocks[first, half], blocks[second, half]], axis=0), pick[s])
-            for t in range(TERMS):
-                scale = jnp.concatenate([chosen[t * 64:t * 64 + 64], chosen[128 + t * 64:192 + t * 64]], axis=0)
-                part = scale * product[:, t * LANES:(t + 1) * LANES]
-                total = part if total is None else total + part
-        return total
+            chosen = dot(jnp.concatenate([blocks[c, half] for c in chunks], axis=0), pick[s])
+            for m in range(n):
+                for t in range(TERMS):
+                    scale = chosen[(m * TERMS + t) * CHUNK:(m * TERMS + t + 1) * CHUNK]
+                    part = scale * product[m * CHUNK:(m + 1) * CHUNK, t * LANES:(t + 1) * LANES]
+                    totals[m] = part if totals[m] is None else totals[m] + part
+        return totals
 
     def right(half, k, sub):
         target = up_two if k in (1, 3, 5) else up
@@ -248,34 +248,43 @@
     def left(half, k, sub):
         target = down_two if k in (0, 2, 4) else down
         return remote(give_l.at[half, k, sub], take_l.at[half, k, sub], l_send.at[half, k, sub], l_recv.at[half, k, sub], target)
+
+    def pass_on(half, k, move, give, take):
+        for sub in range(2):
+            move(half, k - 1, sub).wait_recv()
+            value = give[half, k, sub] + take[half, k - 1, sub]
+            if k >= 2 + k % 2:
+                move(half, k - 2, sub).wait_recv()
+                value = value + take[half, k - 2, sub]
+            give[half, k, sub] = value
+            move(half, k, sub).start()
 
     def reduce_half(half, carry):
         pltpu.make_async_copy(rows_for(half, me), slab(half, (o, i)), own_sem.at[2 + half]).wait()
         for n, source in enumerate(sources):
             remote(rows_for(half, me), slab(half, source), w_send.at[half, n], w_recv.at[half, n], source).wait_recv()
-        for k in range(8):
-            total = chunk_pair(half, rem(z + 8 - k + NZ, NZ), rem(z + 9 + k, NZ))
-            raw, chain = (right, left) if k % 2 == 0 else (left, right)
-            give, take = (give_l, take_l) if k % 2 == 0 else (give_r, take_r)
-            other = give_r if k % 2 == 0 else give_l
-            raw_rows, chain_rows = (total[:CHUNK], total[CHUNK:]) if k % 2 == 0 else (total[CHUNK:], total[:CHUNK])
+        for step in range(0, 8, 2):
+            terms = chunk_terms(half, [rem(z + 8 - step, NZ), rem(z + 7 - step + NZ, NZ), rem(z + 9 + step, NZ), rem(z + 10 + step, NZ)])
             for sub in range(2):
-                other[half, k, sub] = raw_rows[:, sub * 128:(sub + 1) * 128]
-                if k < 7:
-                    raw(half, k, sub).start()
-            for sub in range(2):
-                value = chain_rows[:, sub * 128:(sub + 1) * 128]
-                if k >= 1:
-                    chain(half, k - 1, sub).wait_recv()
-                    value = value + take[half, k - 1, sub]
-                if k >= 2 and k - 2 >= k % 2:
-                    chain(half, k - 2, sub).wait_recv()
-                    value = value + take[half, k - 2, sub]
-                give[half, k, sub] = value
-                chain(half, k, sub).start()
+                for k in range(2):
+                    give_r[half, step + k, sub] = terms[k][:, sub * 128:(sub + 1) * 128]
+                    give_l[half, step + k, sub] = terms[2 + k][:, sub * 128:(sub + 1) * 128]
+                right(half, step, sub).start()
+                if step < 6:
+                    left(half, step + 1, sub).start()
+                if step == 0:
+                    left(half, 0, sub).start()
+            if step == 0:
+                @pl.when(half == 1)
+                def _():
+                    pass_on(0, 7, right, give_r, take_r)
+            if step > 0:
+                pass_on(half, step - 1, right, give_r, take_r)
+                pass_on(half, step, left, give_l, take_l)
         return carry
 
     lax.fori_loop(0, 2, reduce_half, jnp.int32(0))
+    pass_on(1, 7, right, give_r, take_r)
 
     for half in range(2):
         for sub in range(2):

time: 127 us -> 121 us (0.953)
  Pallas kernels: 123 us -> 118 us
    pallas_call x1, Pallas kernels: 123 us -> 118 us  [shards(): pl.pallas_call(kernel, out_shape=jax.ShapeDtypeStruct((OWN, ROWS), BF16),...]
where the time goes in v4:
time: 121 us; the launch traced here: 119 us
  Pallas kernels  118 us (98%)
  local copies, waits for them, and re-layouts  1.47 us (1%)
    pallas_call x1, Pallas kernels, shards(): pl.pallas_call(kernel, out_shape=jax.ShapeDtypeStruct((OWN, ROWS), BF16),...  118 us

profile of v4, /device:TPU:6, one launch (start us, length us, event | category | flops | bytes accessed | tf_op | source)
XLA Modules:
  0.0 119.2 jit_solution(5987490877021447788)
XLA Ops:
  0.0 117.7 %collision_gain.1 = bf16[32,1024]{1,0:T(8,128)(2,1)} custom-call(s32[16,32]{1,0:T(8,128)} %table.1, bf16[2,1024,1024]{2,1,0:T(8,128)(2,1)} %w_hbm.1, bf16[64,1024]{1,0:T(8,128)(2,1)} %bitcast.4, bf16[2,32,1024]{2,1,0:T(8,128)(2,1)} %bitcast.5), custom_call_target="tpu_custom_call" | custom-call | tf_op jit(solution)/shard_map/collision_gain/pallas_call | solution.py:336
  117.7 1.5 %copy.6 = bf16[1024,32]{0,1:T(8,128)(2,1)} copy(bf16[1024,32]{0,1:T(8,128)(2,1)} %bitcast.3) | data formatting | bytes 131072
